TPU v7x, 32 devices: a whole 2x2x4 slice. The times are simulated.
32 devices in a mesh: blk: 16 (over z, x, core), rep: 2 (over y).
Axes of the slice: x: 2, y: 2, z: 4, core: 2. Of those that a mesh axis runs over, the one named last changes fastest.
Arguments:
- frames: bfloat16 [2, 768, 384], P('rep', 'blk'), may hold values from -600 to 600
- codebook: bfloat16 [16384, 384], P('blk'), may hold values from -2 to 2
Outputs:
- log_total: float32 [2, 768], P('rep', 'blk')
- counts: float32 [16384], P('blk')
- entropy: float32 [], replicated
All inputs are finite; a program needn't handle non-finite values.
Results may differ from a plain program's by a relative error of at most 0.00065.
Values may be sent and summed in bfloat16 or wider, within the bound.
A program may use at most 128 MiB of HBM per device.

v0:
```python
import jax
import jax.numpy as jnp
from jax import lax
from jax.sharding import PartitionSpec as P


def joined(part, axis, combine):
    gathered = jax.tree.map(lambda a: lax.all_gather(a, axis), part)

    def take(source):
        return jax.tree.map(lambda a: lax.dynamic_index_in_dim(a, source, 0, False), gathered)

    return lax.fori_loop(
        1, lax.axis_size(axis), lambda source, state: combine(state, take(source)), take(0)
    )


def score_block(moving, codebook):
    return lax.dot_general(
        moving, codebook, (((1,), (1,)), ((), ())), preferred_element_type=jnp.float32
    )


def merge_stats(earlier, later):
    new_high = jnp.maximum(earlier[0], later[0])
    new_total = earlier[1] * jnp.exp(earlier[0] - new_high) + later[1] * jnp.exp(
        later[0] - new_high
    )
    return (new_high, new_total)


def entropy_part(usage, frames_total):
    mean_use = usage / frames_total
    return -jnp.sum(mean_use * jnp.log(mean_use + 1e-07))


def per_device(frames, codebook):
    frame_rows = frames[0]
    shard_rows = frame_rows.shape[0]
    cycle_size = lax.axis_size("blk")
    cycle_index = lax.axis_index("blk")
    group_rows = shard_rows * cycle_size
    scores = score_block(lax.all_gather(frame_rows, "blk", axis=0, tiled=True), codebook)
    local_high = jnp.max(scores, axis=1)
    local_total = jnp.sum(jnp.exp(scores - local_high[:, None]), axis=1)
    row_high, row_total = joined((local_high, local_total), "blk", merge_stats)
    lse_all = row_high + jnp.log(row_total)
    lse_own = lax.dynamic_slice_in_dim(lse_all, cycle_index * shard_rows, shard_rows, 0)
    usage_part = jnp.sum(jnp.exp(scores - lse_all[:, None]), axis=0)
    frames_total = group_rows * lax.axis_size("rep")
    usage = lax.psum(usage_part, "rep")
    entropy = lax.psum(entropy_part(usage, frames_total), "blk")
    return (lse_own[None, :], usage, entropy)


def solution(mesh):
    in_specs = (P("rep", "blk", None), P("blk", None))
    out_specs = (P("rep", "blk"), P("blk"), P())
    return jax.shard_map(
        per_device, mesh=mesh, in_specs=in_specs, out_specs=out_specs, check_vma=False
    )
```

profile of v0, /device:TPU:0, one launch (start us, length us, event | category | flops | bytes accessed | tf_op | source)
XLA Modules:
  0.0 106.4 jit_solution(5990612232053927970)
XLA Ops:
  0.6 0.0 copy-start
  0.6 25.2 %all-gather = bf16[1,768,384]{2,1,0:T(8,128)(2,1)S(1)} all-gather(bf16[1,48,384]{2,1,0:T(8,128)(2,1)} %param.4), channel_id=2, replica_groups=mesh['blk'=16,'rep'=2] {'blk'}, dimensions={1}, use_global_device_ids=true | all-gather | bytes 626688 | tf_op jit(solution)/shard_map/all_gather | solution.py:43
  25.9 0.0 copy-done
  25.9 1.1 %fusion.2 = (f32[768]{0:T(1024)S(1)}, f32[768,1024]{1,0:T(8,128)S(1)}) fusion(bf16[1024,384]{1,0:T(8,128)(2,1)S(1)} %copy-done, bf16[1,768,384]{2,1,0:T(8,128)(2,1)S(1)} %all-gather), kind=kOutput, calls=%fused_computation.14 | convolution fusion | flops 604765440 | bytes 4525056 | tf_op jit(solution)/shard_map/dot_general | solution.py:19
  27.0 0.0 copy-start.1
  27.0 1.7 %copy-done.1 = f32[768,1024]{1,0:T(8,128)} copy-done((f32[768,1024]{1,0:T(8,128)}, f32[768,1024]{1,0:T(8,128)S(1)}, u32[]{:S(2)}) %copy-start.1) | copy-done | bytes 3145752
  28.6 0.9 exponential_reduce_fusion.1
  29.6 17.6 %all-gather.4 = f32[16,1,768]{2,1,0:T(1,128)S(1)} all-gather(f32[1,1,768]{2,1,0:T(1,128)S(1)} %reshape.17), channel_id=4, replica_groups=mesh['blk'=16,'rep'=2] {'blk'}, dimensions={0}, use_global_device_ids=true | all-gather | bytes 52224 | tf_op jit(solution)/shard_map/all_gather | solution.py:8
  47.2 18.9 %all-gather.3 = f32[16,1,768]{2,1,0:T(1,128)S(1)} all-gather(f32[1,1,768]{2,1,0:T(1,128)S(1)} %reshape.15), channel_id=3, replica_groups=mesh['blk'=16,'rep'=2] {'blk'}, dimensions={0}, use_global_device_ids=true | all-gather | bytes 52224 | tf_op jit(solution)/shard_map/all_gather | solution.py:8
  66.1 1.1 %while.17 = (s32[]{:T(128)}, f32[768]{0:T(1024)S(1)}, f32[768]{0:T(1024)S(1)}, f32[16,768]{1,0:T(8,128)S(1)}, f32[16,768]{1,0:T(8,128)S(1)}, /*index=5*/s32[]{:T(128)}, s32[]{:T(128)}, s32[]{:T(128)}) while((s32[]{:T(128)}, f32[768]{0:T(1024)S(1)}, f32[768]{0:T(1024)S(1)}, f32[16,768]{1,0:T(8,128)S(1)}, f32[16,768]{1,0:T(8,128)S(1)}, ...), condition=%wide.region_3.4_spmd, body=%wide.region_2.3_spmd.sunk | while | flops 4613 | bytes 30851 | solution.py:13
  67.2 0.6 dynamic-slice_bitcast_fusion
  67.8 2.4 %exponential_reduce_fusion = f32[1024]{0:T(1024)S(1)} fusion(f32[768,1024]{1,0:T(8,128)} %copy-done.1, f32[768]{0:T(1024)S(1)} %log_add_fusion), kind=kLoop, calls=%fused_computation.3 | loop fusion | flops 1571840 | bytes 3152896 | tf_op jit(solution)/shard_map/reduce_sum | solution.py:49
  70.2 4.9 %psum.14 = f32[1024]{0:T(1024)S(1)} all-reduce(f32[1024]{0:T(1024)S(1)} %exponential_reduce_fusion), channel_id=1, replica_groups=mesh['blk'=16,'rep'=2] {'rep'}, use_global_device_ids=true, to_apply=%region_5.6 | all-reduce | flops 1024 | bytes 8192 | tf_op jit(solution)/shard_map/psum | solution.py:51
  75.1 0.0 copy-start.2
  75.1 0.6 multiply_reduce_fusion
  76.4 30.0 %psum.15 = f32[]{:T(128)} all-reduce(f32[]{:T(128)S(6)} %neg.3), channel_id=1, replica_groups=mesh['blk'=16,'rep'=2] {'blk'}, use_global_device_ids=true, to_apply=%region_7.8 | all-reduce | flops 1 | bytes 8 | tf_op jit(solution)/shard_map/psum | solution.py:52
  106.4 0.0 copy-done.2
  (37 shorter events, 0.7 us)
Async XLA Ops:
  0.6 25.2 %copy-start = (bf16[1024,384]{1,0:T(8,128)(2,1)S(1)}, bf16[1024,384]{1,0:T(8,128)(2,1)}, u32[]{:S(2)}) copy-start(bf16[1024,384]{1,0:T(8,128)(2,1)} %param.5) | copy-start | bytes 2359300
  27.0 1.7 %copy-start.1 = (f32[768,1024]{1,0:T(8,128)}, f32[768,1024]{1,0:T(8,128)S(1)}, u32[]{:S(2)}) copy-start(f32[768,1024]{1,0:T(8,128)S(1)} %get-tuple-element.153) | copy-start | bytes 9437188
  75.1 31.3 %copy-start.2 = (f32[1024]{0:T(1024)}, f32[1024]{0:T(1024)S(1)}, u32[]{:S(2)}) copy-start(f32[1024]{0:T(1024)S(1)} %psum.14) | copy-start | bytes 12292
where the time goes:
time: 107 us; the launch traced here: 106 us
  blocking collectives  96.6 us (90%)
  other arithmetic  4.08 us (4%)
  local copies, waits for them, and re-layouts  2.75 us (3%)
  between operations  1.35 us (1%)
  matrix products  1.09 us (1%)
    all_gather x2, blocking collectives, joined(): gathered = jax.tree.map(lambda a: lax.all_gather(a, axis), part)  36.5 us
    psum x1, blocking collectives, per_device(): entropy = lax.psum(entropy_part(usage, frames_total), 'blk')  30 us
    all_gather x1, blocking collectives, per_device(): lax.all_gather(frame_rows, 'blk', axis=0, tiled=True)  25.2 us
    psum x1, blocking collectives, per_device(): usage = lax.psum(usage_part, 'rep')  4.94 us
    reduce_sum x1, other arithmetic, per_device(): usage_part = jnp.sum(jnp.exp(scores - lse_all[:, None]), axis=0)  2.37 us

commit v1 on v0

v1 whole, which is shorter than its diff:
```python
import functools

import jax
import jax.numpy as jnp
from jax import lax
from jax.experimental import pallas as pl
from jax.experimental.pallas import tpu as pltpu
from jax.sharding import PartitionSpec as P

MESH = pl.DeviceIdType.MESH
LANES = 128
TILES = 4


def each(count, body):
    if count <= 16:
        for i in range(count):
            body(i)
    else:

        def step(i, carry):
            body(i)
            return carry

        lax.fori_loop(0, count, step, 0)


def kernel(
    n,
    reps,
    frame_ref,
    code_hbm,
    lse_ref,
    use_ref,
    ent_ref,
    code,
    fr,
    exps,
    high,
    stats,
    uses,
    terms,
    code_sem,
    fr_send,
    fr_recv,
    st_send,
    st_recv,
    us_send,
    us_recv,
    te_send,
    te_recv,
):
    depth_z = n // 4
    half = n // 2
    block = frame_ref.shape[1]
    protos = code.shape[0]
    vt = protos // TILES
    width = stats.shape[-1]
    lw = 384 if width % 384 == 0 else width
    groups = width // lw
    me = lax.axis_index("blk")
    rep = lax.axis_index("rep")
    c = me % 2
    x = (me // 2) % 2
    z = me // 4

    def dev(zz, xx, cc):
        return (zz * 2 + xx) * 2 + cc

    def pos(xx, cc, zz):
        return xx * half + cc * depth_z + zz

    def rows(p):
        return pl.ds(pl.multiple_of(p * block, block), block)

    upper = z // (depth_z // 2)
    mirrored = z + upper * (depth_z - 1 - 2 * z)

    def near(j):
        jj = j + (depth_z + j - mirrored) // depth_z
        return jj + upper * (depth_z - 1 - 2 * jj)

    load = pltpu.make_async_copy(code_hbm, code, code_sem)
    load.start()

    barrier = pltpu.get_barrier_semaphore()

    def greet(k):
        pl.semaphore_signal(
            barrier, inc=1, device_id={"blk": (me + k + 1) % n}, device_id_type=MESH
        )

    def greet_rep(k):
        pl.semaphore_signal(
            barrier, inc=1, device_id={"rep": (rep + k + 1) % reps}, device_id_type=MESH
        )

    each(n - 1, greet)
    each(reps - 1, greet_rep)
    pl.semaphore_wait(barrier, n - 1 + reps - 1)

    def frame_copy(src, p, target, slot):
        return pltpu.make_async_remote_copy(
            src_ref=src,
            dst_ref=fr.at[rows(p)],
            send_sem=fr_send.at[slot],
            recv_sem=fr_recv.at[p],
            device_id={"blk": target},
            device_id_type=MESH,
        )

    own = pos(x, c, z)
    mine = frame_ref.at[0]
    x_peer = dev(z, 1 - x, c)
    c_peer = dev(z, x, 1 - c)
    to_z, to_x, to_c = 0, depth_z, 2 * depth_z

    each(depth_z - 1, lambda j: frame_copy(mine, own, dev(near(j), x, c), to_z + j).start())
    frame_copy(mine, own, x_peer, to_x).start()
    frame_copy(mine, own, c_peer, to_c).start()
    fr[rows(own), :] = frame_ref[0]

    def arrived(p):
        frame_copy(fr.at[rows(p)], p, me, 0).wait_recv()

    def relay(j):
        p = pos(x, c, near(j))
        arrived(p)
        frame_copy(fr.at[rows(p)], p, x_peer, to_x + 1 + j).start()
        frame_copy(fr.at[rows(p)], p, c_peer, to_c + 1 + j).start()

    each(depth_z - 1, relay)
    each(depth_z, lambda j: arrived(pos(x, 1 - c, j)))
    load.wait()

    def by_group(body):
        if groups == 1:
            body(0)
        else:

            def step(g, carry):
                body(g * lw)
                return carry

            lax.fori_loop(0, groups, step, 0)

    def score(ch, side, t):
        def body(start):
            first = side * (half * block) + start
            moving = fr[pl.ds(pl.multiple_of(first, block), lw), :]
            s = lax.dot_general(
                code[t * vt : (t + 1) * vt, :],
                moving,
                (((1,), (1,)), ((), ())),
                preferred_element_type=jnp.float32,
            )
            at = pl.ds(start, lw) if groups == 1 else pl.ds(pl.multiple_of(start, LANES), lw)
            exps[ch, t * vt : (t + 1) * vt, at] = s
            top = jnp.max(s.reshape(vt // 8, 8, lw), axis=0)
            high[ch, :, at] = top if t == 0 else jnp.maximum(high[ch, :, at], top)

        by_group(body)

    def soften(ch, side):
        def body(start):
            at = pl.ds(start, lw) if groups == 1 else pl.ds(pl.multiple_of(start, LANES), lw)
            top = jnp.max(high[ch, :, at], axis=0, keepdims=True)
            total = jnp.zeros((8, lw), jnp.float32)
            for t in range(TILES):
                e = jnp.exp(exps[ch, t * vt : (t + 1) * vt, at] - top)
                exps[ch, t * vt : (t + 1) * vt, at] = e
                total = total + jnp.sum(e.reshape(vt // 8, 8, lw), axis=0)
            high[ch, 0:1, at] = top
            stats[me, side, :, at] = top + jnp.log(jnp.sum(total, axis=0, keepdims=True))

        by_group(body)

    def stat_copy(ch, side, source, target, k):
        return pltpu.make_async_remote_copy(
            src_ref=stats.at[source, side],
            dst_ref=stats.at[source, side],
            send_sem=st_send.at[ch, k],
            recv_sem=st_recv.at[source, side],
            device_id={"blk": target},
            device_id_type=MESH,
        )

    def tell(ch, side):
        each(n - 1, lambda k: stat_copy(ch, side, me, (me + k + 1) % n, k).start())

    other = 1 - x
    per_tile = depth_z // TILES

    def relay_x(j):
        p = pos(other, c, z) if isinstance(j, int) and j == 0 else pos(other, c, near(j - 1))
        arrived(p)
        frame_copy(fr.at[rows(p)], p, c_peer, to_c + depth_z + j).start()

    for t in range(TILES):
        score(0, x, t)
        for j in range(t * per_tile, (t + 1) * per_tile):
            relay_x(j)
    soften(0, x)
    tell(0, x)

    each(depth_z, lambda j: arrived(pos(other, 1 - c, j)))
    for t in range(TILES):
        score(1, other, t)
    soften(1, other)
    tell(1, other)

    def merged(side, at):
        parts = stats[:, side, :, at]
        top = jnp.max(parts, axis=0)
        return top + jnp.log(jnp.sum(jnp.exp(parts - top[None]), axis=0))

    folded = [None] * TILES
    for ch, side in ((0, x), (1, other)):
        each(n - 1, lambda k: stat_copy(ch, side, (me + k + 1) % n, me, 0).wait_recv())
        for g in range(groups):
            at = pl.ds(g * lw, lw)
            lse = merged(side, at)
            if ch == 0:
                high[0, 1:2, at] = lse
            w = jnp.exp(high[ch, 0:1, at] - lse)
            for t in range(TILES):
                for q in range(lw // LANES):
                    cols = pl.ds(g * lw + q * LANES, LANES)
                    term = exps[ch, t * vt : (t + 1) * vt, cols] * w[:, q * LANES : (q + 1) * LANES]
                    folded[t] = term if folded[t] is None else folded[t] + term

    ones = jnp.ones((8, LANES), jnp.float32)
    for t in range(TILES):
        part = lax.dot_general(
            ones,
            folded[t],
            (((1,), (1,)), ((), ())),
            precision=lax.Precision.HIGHEST,
            preferred_element_type=jnp.float32,
        )
        uses[rep, :, t * vt : (t + 1) * vt] = part[0:1, :]

    def use_copy(source, target, k):
        return pltpu.make_async_remote_copy(
            src_ref=uses.at[source],
            dst_ref=uses.at[source],
            send_sem=us_send.at[k],
            recv_sem=us_recv.at[source],
            device_id={"rep": target},
            device_id_type=MESH,
        )

    each(reps - 1, lambda k: use_copy(rep, (rep + k + 1) % reps, k).start())

    shift = (c * depth_z + z) * block
    row = jnp.broadcast_to(high[0, 1:2, :], (8, width))
    lse_ref[...] = pltpu.roll(row, (width - shift) % width, 1)[0:1, 0:block]

    each(reps - 1, lambda k: use_copy((rep + k + 1) % reps, rep, k).wait_recv())
    usage = uses[0]
    for k in range(1, reps):
        usage = usage + uses[k]
    use_ref[...] = usage
    mean_use = usage / jnp.float32(n * block * reps)
    term = -jnp.sum(mean_use * jnp.log(mean_use + 1e-07), axis=1, keepdims=True)
    terms[me] = jnp.broadcast_to(term, (1, LANES))

    def term_copy(source, target, k):
        return pltpu.make_async_remote_copy(
            src_ref=terms.at[source],
            dst_ref=terms.at[source],
            send_sem=te_send.at[k],
            recv_sem=te_recv.at[source],
            device_id={"blk": target},
            device_id_type=MESH,
        )

    each(n - 1, lambda k: term_copy(me, (me + k + 1) % n, k).start())

    each(depth_z - 1, lambda s: frame_copy(mine, own, me, to_z + s).wait_send())
    each(3 * depth_z, lambda s: frame_copy(mine, own, me, to_x + s).wait_send())
    for ch, side in ((0, x), (1, other)):
        each(n - 1, lambda k: stat_copy(ch, side, me, me, k).wait_send())
    each(reps - 1, lambda k: use_copy(rep, rep, k).wait_send())

    each(n - 1, lambda k: term_copy((me + k + 1) % n, me, 0).wait_recv())
    ent_ref[0, 0] = jnp.sum(terms[...], axis=0)[0, 0]
    each(n - 1, lambda k: term_copy(me, me, k).wait_send())


def per_device(n, reps, frames, codebook):
    block = frames.shape[1]
    protos, depth = codebook.shape
    width = n // 2 * block
    dz = n // 4
    dma = pltpu.SemaphoreType.DMA
    lse, usage, entropy = pl.pallas_call(
        functools.partial(kernel, n, reps),
        out_shape=(
            jax.ShapeDtypeStruct((1, block), jnp.float32),
            jax.ShapeDtypeStruct((1, protos), jnp.float32),
            jax.ShapeDtypeStruct((1, 1), jnp.float32),
        ),
        in_specs=[
            pl.BlockSpec(memory_space=pltpu.VMEM),
            pl.BlockSpec(memory_space=pl.ANY),
        ],
        out_specs=(
            pl.BlockSpec(memory_space=pltpu.VMEM),
            pl.BlockSpec(memory_space=pltpu.VMEM),
            pl.BlockSpec(memory_space=pltpu.SMEM),
        ),
        scratch_shapes=[
            pltpu.VMEM((protos, depth), jnp.bfloat16),
            pltpu.VMEM((n * block, depth), jnp.bfloat16),
            pltpu.VMEM((2, protos, width), jnp.float32),
            pltpu.VMEM((2, 8, width), jnp.float32),
            pltpu.VMEM((n, 2, 1, width), jnp.float32),
            pltpu.VMEM((reps, 1, protos), jnp.float32),
            pltpu.VMEM((n, 1, LANES), jnp.float32),
            dma,
            dma((4 * dz,)),
            dma((n,)),
            dma((2, n)),
            dma((n, 2)),
            dma((reps,)),
            dma((reps,)),
            dma((n,)),
            dma((n,)),
        ],
        compiler_params=pltpu.CompilerParams(collective_id=0, has_side_effects=True),
    )(frames, codebook)
    return lse, usage.reshape(protos), entropy.reshape(())


def solution(mesh):
    sizes = dict(mesh.shape)
    return jax.shard_map(
        functools.partial(per_device, sizes["blk"], sizes["rep"]),
        mesh=mesh,
        in_specs=(P("rep", "blk", None), P("blk", None)),
        out_specs=(P("rep", "blk"), P("blk"), P()),
        check_vma=False,
    )
```

time: 107 us -> 34.2 us (0.32)
  blocking collectives: 96.6 us -> 0 us
  Pallas kernels: 0 us -> 29.8 us
  other arithmetic: 4.08 us -> 0 us
  matrix products: 1.09 us -> 0 us
    all_gather x3 -> x0, blocking collectives: 61.7 us -> none  [the longest x2 36.5 us: joined(): gathered = jax.tree.map(lambda a: lax.all_gather(a, axis), part)]
    psum x2 -> x0, blocking collectives: 34.9 us -> none  [the longest x1 30 us: per_device(): entropy = lax.psum(entropy_part(usage, frames_total), 'blk')]
    pallas_call x0 -> x1, Pallas kernels: none -> 29.8 us  [per_device(): pl.pallas_call(functools.partial(kernel, n, reps), out_shape=(jax.ShapeDt...]
    reduce_sum x3 -> x0, other arithmetic: 3.9 us -> none  [the longest x1 2.37 us: per_device(): usage_part = jnp.sum(jnp.exp(scores - lse_all[:, None]), axis=0)]
    dot_general x1 -> x0, matrix products: 1.09 us -> none  [score_block(): lax.dot_general(moving, codebook, (((1,), (1,)), ((), ())), preferred_ele...]
where the time goes in v1:
time: 34.2 us; the launch traced here: 34 us
  Pallas kernels  29.8 us (87%)
  between operations  2.4 us (7%)
  local copies, waits for them, and re-layouts  1.74 us (5%)
    pallas_call x1, Pallas kernels, per_device(): pl.pallas_call(functools.partial(kernel, n, reps), out_shape=(jax.ShapeDt...  29.8 us
    unnamed x6, local copies, waits for them, and re-layouts  1.74 us

profile of v1, /device:TPU:0, one launch (start us, length us, event | category | flops | bytes accessed | tf_op | source)
XLA Modules:
  0.0 34.0 jit_solution(16117722306513569900)
XLA Ops:
  0.6 29.8 %shard_map.49 = (f32[1,48]{1,0:T(1,128)}, f32[1,1024]{1,0:T(1,128)}, f32[1,1]{1,0:T(1,128)}) custom-call(bf16[1,48,384]{2,1,0:T(8,128)(2,1)} %frame_ref.1, bf16[1024,384]{1,0:T(8,128)(2,1)} %code_hbm.1), custom_call_target="tpu_custom_call" | custom-call | tf_op jit(solution)/shard_map/pallas_call | solution.py:297
  30.5 0.0 copy-start
  30.5 0.0 copy-start.1
  30.5 0.6 %copy-done.1 = f32[1,48]{1,0:T(1,128)S(1)} copy-done((f32[1,48]{1,0:T(1,128)S(1)}, f32[1,48]{1,0:T(1,128)}, u32[]{:S(2)}) %copy-start.1) | copy-done | bytes 216
  31.1 0.5 %copy.8 = f32[1,48]{1,0:T(1,128)} copy(f32[1,48]{1,0:T(1,128)S(1)} %copy-done.1) | data formatting | bytes 384
  31.6 0.0 copy-done
  31.6 0.6 %copy.9 = f32[1024]{0:T(1024)} copy(f32[1024]{0:T(1024)S(1)} %bitcast.2) | data formatting | bytes 8192
Async XLA Ops:
  30.5 1.2 %copy-start = (f32[1,1024]{1,0:T(1,128)S(1)}, f32[1,1024]{1,0:T(1,128)}, u32[]{:S(2)}) copy-start(f32[1,1024]{1,0:T(1,128)} %get-tuple-element.7) | copy-start | bytes 12292
  30.5 0.6 %copy-start.1 = (f32[1,48]{1,0:T(1,128)S(1)}, f32[1,48]{1,0:T(1,128)}, u32[]{:S(2)}) copy-start(f32[1,48]{1,0:T(1,128)} %get-tuple-element.12) | copy-start | bytes 580

commit v2 on v1

v2 whole, which is shorter than its diff:
```python
import functools

import jax
import jax.numpy as jnp
from jax import lax
from jax.experimental import pallas as pl
from jax.experimental.pallas import tpu as pltpu
from jax.sharding import PartitionSpec as P

MESH = pl.DeviceIdType.MESH
LANES = 128
VT = 256


def each(count, body):
    if count <= 16:
        for i in range(count):
            body(i)
    else:

        def step(i, carry):
            body(i)
            return carry

        lax.fori_loop(0, count, step, 0)


def kernel(
    n,
    reps,
    frame_hbm,
    code_hbm,
    lse_ref,
    use_ref,
    ent_ref,
    code,
    fr,
    exps,
    high,
    stats,
    uses,
    terms,
    code_sem,
    own_sem,
    code_send,
    code_recv,
    fr_send,
    fr_recv,
    st_send,
    st_recv,
    us_send,
    us_recv,
    te_send,
    te_recv,
):
    deep = n // 4
    half = n // 2
    block = frame_hbm.shape[1]
    protos = code.shape[1]
    tiles = protos // VT
    width = stats.shape[-1]
    used = deep * block
    lw = 256 if width % 256 == 0 else width
    groups = width // lw
    me = lax.axis_index("blk")
    rep = lax.axis_index("rep")
    c = me % 2
    x = (me // 2) % 2
    z = me // 4
    q_me = x * deep + z
    other = 1 - x

    def dev(zz, xx, cc):
        return (zz * 2 + xx) * 2 + cc

    def dev_q(q):
        return dev(q % deep, q // deep, c)

    def rows(zz):
        return pl.ds(pl.multiple_of(zz * block, block), block)

    upper = z // (deep // 2)
    mirrored = z + upper * (deep - 1 - 2 * z)

    def near(j):
        jj = j + (deep + j - mirrored) // deep
        return jj + upper * (deep - 1 - 2 * jj)

    x_peer = dev(z, other, c)
    c_peer = dev(z, x, 1 - c)

    barrier = pltpu.get_barrier_semaphore()

    def greet(**where):
        pl.semaphore_signal(barrier, inc=1, device_id=where, device_id_type=MESH)

    each(deep - 1, lambda j: greet(blk=dev(near(j), x, c)))
    greet(blk=x_peer)
    greet(blk=c_peer)
    for k in range(1, reps):
        greet(rep=(rep + k) % reps, blk=me)
        greet(rep=(rep + k) % reps, blk=c_peer)
    own = pltpu.make_async_copy(frame_hbm.at[0], fr.at[x, rows(z)], own_sem)
    own.start()
    load = pltpu.make_async_copy(code_hbm, code.at[c], code_sem)
    load.start()
    if width > used:
        fr[:, used:, :] = jnp.zeros((2, width - used, fr.shape[2]), fr.dtype)
    own.wait()
    pl.semaphore_wait(barrier, deep + 1 + 2 * (reps - 1))

    def frame_copy(xx, zz, target, slot):
        return pltpu.make_async_remote_copy(
            src_ref=fr.at[xx, rows(zz)],
            dst_ref=fr.at[xx, rows(zz)],
            send_sem=fr_send.at[slot],
            recv_sem=fr_recv.at[xx, zz],
            device_id={"blk": target},
            device_id_type=MESH,
        )

    def code_copy(cc, target):
        return pltpu.make_async_remote_copy(
            src_ref=code_hbm,
            dst_ref=code.at[cc],
            send_sem=code_send,
            recv_sem=code_recv,
            device_id={"blk": target},
            device_id_type=MESH,
        )

    each(deep - 1, lambda j: frame_copy(x, z, dev(near(j), x, c), j).start())
    frame_copy(x, z, x_peer, deep).start()
    code_copy(c, c_peer).start()

    def arrived(xx, zz):
        frame_copy(xx, zz, x_peer, 0).wait_recv()

    def relay(j):
        arrived(x, near(j))
        frame_copy(x, near(j), x_peer, deep + 1 + j).start()

    each(deep - 1, relay)

    def by_group(body):
        if groups == 1:
            body(pl.ds(0, lw))
        else:

            def step(g, carry):
                body(pl.ds(pl.multiple_of(g * lw, lw), lw))
                return carry

            lax.fori_loop(0, groups, step, 0)

    def score(ch, side, cc, first):
        def body(at):
            moving = fr[side, at, :]
            top = None
            for t in range(tiles):
                s = lax.dot_general(
                    code[cc, t * VT : (t + 1) * VT, :],
                    moving,
                    (((1,), (1,)), ((), ())),
                    preferred_element_type=jnp.float32,
                )
                exps[ch, cc, t * VT : (t + 1) * VT, at] = s
                peak = jnp.max(s.reshape(VT // 8, 8, lw), axis=0)
                top = peak if top is None else jnp.maximum(top, peak)
            high[ch, :, at] = top if first else jnp.maximum(high[ch, :, at], top)

        by_group(body)

    def soften(ch, side):
        def body(at):
            top = jnp.max(high[ch, :, at], axis=0, keepdims=True)
            total = jnp.zeros((8, lw), jnp.float32)
            for cc in range(2):
                for t in range(tiles):
                    e = jnp.exp(exps[ch, cc, t * VT : (t + 1) * VT, at] - top)
                    exps[ch, cc, t * VT : (t + 1) * VT, at] = e
                    total = total + jnp.sum(e.reshape(VT // 8, 8, lw), axis=0)
            high[ch, 0:1, at] = top
            stats[q_me, side, :, at] = top + jnp.log(jnp.sum(total, axis=0, keepdims=True))

        by_group(body)

    def stat_copy(ch, side, source, target, k):
        return pltpu.make_async_remote_copy(
            src_ref=stats.at[source, side],
            dst_ref=stats.at[source, side],
            send_sem=st_send.at[ch, k],
            recv_sem=st_recv.at[source, side],
            device_id={"blk": target},
            device_id_type=MESH,
        )

    def peer(k):
        return (q_me + k + 1) % half

    def tell(ch, side):
        each(half - 1, lambda k: stat_copy(ch, side, q_me, dev_q(peer(k)), k).start())

    load.wait()
    score(0, x, c, True)
    code_copy(1 - c, c_peer).wait_recv()
    score(0, x, 1 - c, False)
    soften(0, x)
    each(deep, lambda j: arrived(other, j))
    tell(0, x)
    score(1, other, 0, True)
    score(1, other, 1, False)
    soften(1, other)
    tell(1, other)

    def merged(side, at):
        parts = stats[:, side, :, at]
        top = jnp.max(parts, axis=0)
        return top + jnp.log(jnp.sum(jnp.exp(parts - top[None]), axis=0))

    folded = [None] * (2 * tiles)
    for ch, side in ((0, x), (1, other)):
        each(half - 1, lambda k: stat_copy(ch, side, peer(k), x_peer, 0).wait_recv())
        for g in range(groups):
            at = pl.ds(g * lw, lw)
            lse = merged(side, at)
            if ch == 0:
                high[0, 1:2, at] = lse
            w = jnp.exp(high[ch, 0:1, at] - lse)
            if width > used:
                lane = lax.broadcasted_iota(jnp.int32, (1, lw), 1) + g * lw
                w = jnp.where(lane < used, w, 0.0)
            for t in range(2 * tiles):
                for q in range(lw // LANES):
                    e = exps[
                        ch,
                        t // tiles,
                        t % tiles * VT : (t % tiles + 1) * VT,
                        pl.ds(g * lw + q * LANES, LANES),
                    ]
                    part = e * w[:, q * LANES : (q + 1) * LANES]
                    folded[t] = part if folded[t] is None else folded[t] + part

    ones = jnp.ones((8, LANES), jnp.float32)
    here = rep * 2 + c
    for t in range(2 * tiles):
        part = lax.dot_general(
            ones,
            folded[t],
            (((1,), (1,)), ((), ())),
            precision=lax.Precision.HIGHEST,
            preferred_element_type=jnp.float32,
        )
        uses[here, t // tiles, :, t % tiles * VT : (t % tiles + 1) * VT] = part[0:1, :]

    def use_copy(source, target_rep, target, k):
        return pltpu.make_async_remote_copy(
            src_ref=uses.at[source],
            dst_ref=uses.at[source],
            send_sem=us_send.at[k],
            recv_sem=us_recv.at[source],
            device_id={"rep": target_rep, "blk": target},
            device_id_type=MESH,
        )

    for k in range(1, reps):
        to = (rep + k) % reps
        use_copy(here, to, me, 2 * k).start()
        use_copy(here, to, c_peer, 2 * k + 1).start()
    use_copy(here, rep, c_peer, 1).start()

    row = jnp.broadcast_to(high[0, 1:2, :], (8, width))
    lse_ref[...] = pltpu.roll(row, (width - z * block) % width, 1)[0:1, 0:block]

    for k in range(1, 2 * reps):
        use_copy((here + k) % (2 * reps), rep, c_peer, 0).wait_recv()
    usage = uses[0]
    for k in range(1, 2 * reps):
        usage = usage + uses[k]
    uses_own = uses[0, c]
    for k in range(1, 2 * reps):
        uses_own = uses_own + uses[k, c]
    use_ref[...] = uses_own
    mean_use = usage / jnp.float32(n * block * reps)
    term = mean_use * jnp.log(mean_use + 1e-07)
    term = -jnp.sum(term[0] + term[1], axis=1, keepdims=True)
    terms[q_me] = jnp.broadcast_to(term, (1, LANES))

    def term_copy(source, target, k):
        return pltpu.make_async_remote_copy(
            src_ref=terms.at[source],
            dst_ref=terms.at[source],
            send_sem=te_send.at[k],
            recv_sem=te_recv.at[source],
            device_id={"blk": target},
            device_id_type=MESH,
        )

    each(half - 1, lambda k: term_copy(q_me, dev_q(peer(k)), k).start())

    each(deep - 1, lambda s: frame_copy(x, z, x_peer, s).wait_send())
    each(deep, lambda s: frame_copy(x, z, x_peer, deep + s).wait_send())
    code_copy(c, c_peer).wait_send()
    for ch, side in ((0, x), (1, other)):
        each(half - 1, lambda k: stat_copy(ch, side, q_me, x_peer, k).wait_send())
    for k in range(1, 2 * reps):
        use_copy(here, rep, c_peer, k).wait_send()

    each(half - 1, lambda k: term_copy(peer(k), x_peer, 0).wait_recv())
    ent_ref[0, 0] = jnp.sum(terms[...], axis=0)[0, 0]
    each(half - 1, lambda k: term_copy(q_me, x_peer, k).wait_send())


def per_device(n, reps, frames, codebook):
    block = frames.shape[1]
    protos, depth = codebook.shape
    deep, half = n // 4, n // 2
    width = -(-deep * block // LANES) * LANES
    dma = pltpu.SemaphoreType.DMA
    lse, usage, entropy = pl.pallas_call(
        functools.partial(kernel, n, reps),
        out_shape=(
            OUT((1, block), jnp.float32),
            OUT((1, protos), jnp.float32),
            jax.ShapeDtypeStruct((1, 1), jnp.float32),
        ),
        in_specs=[
            pl.BlockSpec(memory_space=pl.ANY),
            pl.BlockSpec(memory_space=pl.ANY),
        ],
        out_specs=(
            pl.BlockSpec(memory_space=pltpu.VMEM),
            pl.BlockSpec(memory_space=pltpu.VMEM),
            pl.BlockSpec(memory_space=pltpu.SMEM),
        ),
        scratch_shapes=[
            pltpu.VMEM((2, protos, depth), jnp.bfloat16),
            pltpu.VMEM((2, width, depth), jnp.bfloat16),
            pltpu.VMEM((2, 2, protos, width), jnp.float32),
            pltpu.VMEM((2, 8, width), jnp.float32),
            pltpu.VMEM((half, 2, 1, width), jnp.float32),
            pltpu.VMEM((2 * reps, 2, 1, protos), jnp.float32),
            pltpu.VMEM((half, 1, LANES), jnp.float32),
            dma,
            dma,
            dma,
            dma,
            dma((2 * deep,)),
            dma((2, deep)),
            dma((2, half)),
            dma((half, 2)),
            dma((2 * reps,)),
            dma((2 * reps,)),
            dma((half,)),
            dma((half,)),
        ],
        compiler_params=pltpu.CompilerParams(collective_id=0, has_side_effects=True),
    )(frames, codebook)
    return lse, usage.reshape(protos), entropy.reshape(())


OUT = pltpu.VMEM


def solution(mesh):
    sizes = dict(mesh.shape)
    return jax.shard_map(
        functools.partial(per_device, sizes["blk"], sizes["rep"]),
        mesh=mesh,
        in_specs=(P("rep", "blk", None), P("blk", None)),
        out_specs=(P("rep", "blk"), P("blk"), P()),
        check_vma=False,
    )
```

time: 34.2 us -> 31.6 us (0.924)
  Pallas kernels: 29.8 us -> 28 us
  local copies, waits for them, and re-layouts: 1.74 us -> 1.11 us
    pallas_call x1, Pallas kernels: 29.8 us -> 28 us  [per_device(): pl.pallas_call(functools.partial(kernel, n, reps), out_shape=(OUT((1, blo...]
    unnamed x6 -> x2, local copies, waits for them, and re-layouts: 1.74 us -> 1.11 us
where the time goes in v2:
time: 31.6 us; the launch traced here: 31.4 us
  Pallas kernels  28 us (89%)
  between operations  2.33 us (7%)
  local copies, waits for them, and re-layouts  1.11 us (4%)
    pallas_call x1, Pallas kernels, per_device(): pl.pallas_call(functools.partial(kernel, n, reps), out_shape=(OUT((1, blo...  28 us
    unnamed x2, local copies, waits for them, and re-layouts  1.11 us

profile of v2, /device:TPU:0, one launch (start us, length us, event | category | flops | bytes accessed | tf_op | source)
XLA Modules:
  0.0 31.4 jit_solution(18340950998304474752)
XLA Ops:
  0.6 28.0 %shard_map.49 = (f32[1,48]{1,0:T(1,128)S(1)}, f32[1,1024]{1,0:T(1,128)S(1)}, f32[1,1]{1,0:T(1,128)}) custom-call(bf16[1,48,384]{2,1,0:T(8,128)(2,1)} %frame_hbm.1, bf16[1024,384]{1,0:T(8,128)(2,1)} %code_hbm.1), custom_call_target="tpu_custom_call" | custom-call | tf_op jit(solution)/shard_map/pallas_call | solution.py:320
  28.6 0.5 %copy.8 = f32[1,48]{1,0:T(1,128)} copy(f32[1,48]{1,0:T(1,128)S(1)} %get-tuple-element.9) | data formatting | bytes 384
  29.1 0.6 %copy.9 = f32[1024]{0:T(1024)} copy(f32[1024]{0:T(1024)S(1)} %bitcast.2) | data formatting | bytes 8192

commit v3 on v2

--- a/solution.py
+++ b/solution.py
@@ -37,6 +37,8 @@
     fr,
     exps,
     high,
+    sums,
+    row_lse,
     stats,
     uses,
     terms,
@@ -129,8 +131,8 @@
             device_id_type=MESH,
         )
 
-    each(deep - 1, lambda j: frame_copy(x, z, dev(near(j), x, c), j).start())
     frame_copy(x, z, x_peer, deep).start()
+    each(deep - 1, lambda j: frame_copy(x, z, dev(near(deep - 2 - j), x, c), j).start())
     code_copy(c, c_peer).start()
 
     def arrived(xx, zz):
@@ -153,35 +155,31 @@
 
             lax.fori_loop(0, groups, step, 0)
 
-    def score(ch, side, cc, first):
+    def score(ch, side, cc):
         def body(at):
             moving = fr[side, at, :]
-            top = None
             for t in range(tiles):
+                row = cc * tiles + t
                 s = lax.dot_general(
                     code[cc, t * VT : (t + 1) * VT, :],
                     moving,
                     (((1,), (1,)), ((), ())),
                     preferred_element_type=jnp.float32,
                 )
-                exps[ch, cc, t * VT : (t + 1) * VT, at] = s
-                peak = jnp.max(s.reshape(VT // 8, 8, lw), axis=0)
-                top = peak if top is None else jnp.maximum(top, peak)
-            high[ch, :, at] = top if first else jnp.maximum(high[ch, :, at], top)
+                peak = jnp.max(s, axis=0, keepdims=True)
+                e = jnp.exp(s - peak)
+                exps[ch, cc, t * VT : (t + 1) * VT, at] = e
+                high[ch, pl.ds(row, 1), at] = peak
+                sums[ch, pl.ds(row, 1), at] = jnp.sum(e, axis=0, keepdims=True)
 
         by_group(body)
 
     def soften(ch, side):
         def body(at):
-            top = jnp.max(high[ch, :, at], axis=0, keepdims=True)
-            total = jnp.zeros((8, lw), jnp.float32)
-            for cc in range(2):
-                for t in range(tiles):
-                    e = jnp.exp(exps[ch, cc, t * VT : (t + 1) * VT, at] - top)
-                    exps[ch, cc, t * VT : (t + 1) * VT, at] = e
-                    total = total + jnp.sum(e.reshape(VT // 8, 8, lw), axis=0)
-            high[ch, 0:1, at] = top
-            stats[q_me, side, :, at] = top + jnp.log(jnp.sum(total, axis=0, keepdims=True))
+            peaks = high[ch, :, at]
+            top = jnp.max(peaks, axis=0, keepdims=True)
+            total = jnp.sum(sums[ch, :, at] * jnp.exp(peaks - top), axis=0, keepdims=True)
+            stats[q_me, side, :, at] = top + jnp.log(total)
 
         by_group(body)
 
@@ -202,14 +200,14 @@
         each(half - 1, lambda k: stat_copy(ch, side, q_me, dev_q(peer(k)), k).start())
 
     load.wait()
-    score(0, x, c, True)
+    score(0, x, c)
     code_copy(1 - c, c_peer).wait_recv()
-    score(0, x, 1 - c, False)
+    score(0, x, 1 - c)
     soften(0, x)
     each(deep, lambda j: arrived(other, j))
     tell(0, x)
-    score(1, other, 0, True)
-    score(1, other, 1, False)
+    score(1, other, 0)
+    score(1, other, 1)
     soften(1, other)
     tell(1, other)
 
@@ -225,8 +223,8 @@
             at = pl.ds(g * lw, lw)
             lse = merged(side, at)
             if ch == 0:
-                high[0, 1:2, at] = lse
-            w = jnp.exp(high[ch, 0:1, at] - lse)
+                row_lse[:, at] = lse
+            w = jnp.exp(high[ch, :, at] - lse)
             if width > used:
                 lane = lax.broadcasted_iota(jnp.int32, (1, lw), 1) + g * lw
                 w = jnp.where(lane < used, w, 0.0)
@@ -238,17 +236,20 @@
                         t % tiles * VT : (t % tiles + 1) * VT,
                         pl.ds(g * lw + q * LANES, LANES),
                     ]
-                    part = e * w[:, q * LANES : (q + 1) * LANES]
+                    part = e * w[t : t + 1, q * LANES : (q + 1) * LANES]
                     folded[t] = part if folded[t] is None else folded[t] + part
 
-    ones = jnp.ones((8, LANES), jnp.float32)
+    ones = jnp.ones((8, 3 * LANES), jnp.bfloat16)
     here = rep * 2 + c
     for t in range(2 * tiles):
+        big = folded[t].astype(jnp.bfloat16)
+        rest = folded[t] - big.astype(jnp.float32)
+        mid = rest.astype(jnp.bfloat16)
+        low = (rest - mid.astype(jnp.float32)).astype(jnp.bfloat16)
         part = lax.dot_general(
             ones,
-            folded[t],
+            jnp.concatenate([big, mid, low], axis=1),
             (((1,), (1,)), ((), ())),
-            precision=lax.Precision.HIGHEST,
             preferred_element_type=jnp.float32,
         )
         uses[here, t // tiles, :, t % tiles * VT : (t % tiles + 1) * VT] = part[0:1, :]
@@ -269,7 +270,7 @@
         use_copy(here, to, c_peer, 2 * k + 1).start()
     use_copy(here, rep, c_peer, 1).start()
 
-    row = jnp.broadcast_to(high[0, 1:2, :], (8, width))
+    row = jnp.broadcast_to(row_lse[...], (8, width))
     lse_ref[...] = pltpu.roll(row, (width - z * block) % width, 1)[0:1, 0:block]
 
     for k in range(1, 2 * reps):
@@ -337,7 +338,9 @@
             pltpu.VMEM((2, protos, depth), jnp.bfloat16),
             pltpu.VMEM((2, width, depth), jnp.bfloat16),
             pltpu.VMEM((2, 2, protos, width), jnp.float32),
-            pltpu.VMEM((2, 8, width), jnp.float32),
+            pltpu.VMEM((2, 2 * (protos // VT), width), jnp.float32),
+            pltpu.VMEM((2, 2 * (protos // VT), width), jnp.float32),
+            pltpu.VMEM((1, width), jnp.float32),
             pltpu.VMEM((half, 2, 1, width), jnp.float32),
             pltpu.VMEM((2 * reps, 2, 1, protos), jnp.float32),
             pltpu.VMEM((half, 1, LANES), jnp.float32),

time: 31.6 us -> 30.4 us (0.962)
  Pallas kernels: 28 us -> 26.8 us
    pallas_call x1, Pallas kernels: 28 us -> 26.8 us  [per_device(): pl.pallas_call(functools.partial(kernel, n, reps), out_shape=(OUT((1, blo...]
where the time goes in v3:
time: 30.4 us; the launch traced here: 30.3 us
  Pallas kernels  26.8 us (88%)
  between operations  2.33 us (8%)
  local copies, waits for them, and re-layouts  1.11 us (4%)
    pallas_call x1, Pallas kernels, per_device(): pl.pallas_call(functools.partial(kernel, n, reps), out_shape=(OUT((1, blo...  26.8 us
    unnamed x2, local copies, waits for them, and re-layouts  1.11 us

profile of v3, /device:TPU:0, one launch (start us, length us, event | category | flops | bytes accessed | tf_op | source)
XLA Modules:
  0.0 30.3 jit_solution(12050587439979427265)
XLA Ops:
  0.6 26.8 %shard_map.49 = (f32[1,48]{1,0:T(1,128)S(1)}, f32[1,1024]{1,0:T(1,128)S(1)}, f32[1,1]{1,0:T(1,128)}) custom-call(bf16[1,48,384]{2,1,0:T(8,128)(2,1)} %frame_hbm.1, bf16[1024,384]{1,0:T(8,128)(2,1)} %code_hbm.1), custom_call_target="tpu_custom_call" | custom-call | tf_op jit(solution)/shard_map/pallas_call | solution.py:321
  27.5 0.5 %copy.8 = f32[1,48]{1,0:T(1,128)} copy(f32[1,48]{1,0:T(1,128)S(1)} %get-tuple-element.9) | data formatting | bytes 384
  28.0 0.6 %copy.9 = f32[1024]{0:T(1024)} copy(f32[1024]{0:T(1024)S(1)} %bitcast.2) | data formatting | bytes 8192

commit v4 on v3

--- a/solution.py
+++ b/solution.py
@@ -54,6 +54,7 @@
     us_recv,
     te_send,
     te_recv,
+    up_ready,
 ):
     deep = n // 4
     half = n // 2
@@ -81,13 +82,6 @@
     def rows(zz):
         return pl.ds(pl.multiple_of(zz * block, block), block)
 
-    upper = z // (deep // 2)
-    mirrored = z + upper * (deep - 1 - 2 * z)
-
-    def near(j):
-        jj = j + (deep + j - mirrored) // deep
-        return jj + upper * (deep - 1 - 2 * jj)
-
     x_peer = dev(z, other, c)
     c_peer = dev(z, x, 1 - c)
 
@@ -96,7 +90,13 @@
     def greet(**where):
         pl.semaphore_signal(barrier, inc=1, device_id=where, device_id_type=MESH)
 
-    each(deep - 1, lambda j: greet(blk=dev(near(j), x, c)))
+    def above(j, body):
+        pl.when(z + 1 + j < deep)(lambda: body(z + 1 + j))
+
+    def below(j, body):
+        pl.when(j < z)(lambda: body(z - 1 - j))
+
+    each(deep - 1, lambda j: above(j, lambda zz: greet(blk=dev(zz, x, c))))
     greet(blk=x_peer)
     greet(blk=c_peer)
     for k in range(1, reps):
@@ -109,13 +109,20 @@
     if width > used:
         fr[:, used:, :] = jnp.zeros((2, width - used, fr.shape[2]), fr.dtype)
     own.wait()
-    pl.semaphore_wait(barrier, deep + 1 + 2 * (reps - 1))
-
-    def frame_copy(xx, zz, target, slot):
+    pl.semaphore_wait(barrier, z + 2 + 2 * (reps - 1))
+
+    def ready(zz):
+        pl.semaphore_signal(
+            up_ready.at[z], inc=1, device_id={"blk": dev(zz, x, c)}, device_id_type=MESH
+        )
+
+    each(deep - 1, lambda j: pl.when(j < z)(lambda: ready(j)))
+
+    def frame_copy(xx, zz, target, way, slot):
         return pltpu.make_async_remote_copy(
             src_ref=fr.at[xx, rows(zz)],
             dst_ref=fr.at[xx, rows(zz)],
-            send_sem=fr_send.at[slot],
+            send_sem=fr_send.at[way, slot],
             recv_sem=fr_recv.at[xx, zz],
             device_id={"blk": target},
             device_id_type=MESH,
@@ -131,18 +138,30 @@
             device_id_type=MESH,
         )
 
-    frame_copy(x, z, x_peer, deep).start()
-    each(deep - 1, lambda j: frame_copy(x, z, dev(near(deep - 2 - j), x, c), j).start())
+    each(deep - 1, lambda j: pl.when(j < z)(lambda: frame_copy(x, z, dev(j, x, c), 0, j).start()))
+    frame_copy(x, z, x_peer, 1, z).start()
     code_copy(c, c_peer).start()
 
     def arrived(xx, zz):
-        frame_copy(xx, zz, x_peer, 0).wait_recv()
-
-    def relay(j):
-        arrived(x, near(j))
-        frame_copy(x, near(j), x_peer, deep + 1 + j).start()
-
-    each(deep - 1, relay)
+        frame_copy(xx, zz, x_peer, 0, 0).wait_recv()
+
+    def relay(zz):
+        arrived(x, zz)
+        frame_copy(x, zz, x_peer, 1, zz).start()
+
+    def send_up(zz):
+        pl.semaphore_wait(up_ready.at[zz], 1)
+        frame_copy(x, z, dev(zz, x, c), 0, zz).start()
+
+    above(0, send_up)
+    above(1, send_up)
+    each(deep - 1, lambda j: below(j, relay))
+
+    def onward(j):
+        above(j, relay)
+        above(j + 2, send_up)
+
+    each(deep - 1, onward)
 
     def by_group(body):
         if groups == 1:
@@ -299,8 +318,9 @@
 
     each(half - 1, lambda k: term_copy(q_me, dev_q(peer(k)), k).start())
 
-    each(deep - 1, lambda s: frame_copy(x, z, x_peer, s).wait_send())
-    each(deep, lambda s: frame_copy(x, z, x_peer, deep + s).wait_send())
+    each(deep - 1, lambda j: below(j, lambda s: frame_copy(x, z, x_peer, 0, s).wait_send()))
+    each(deep - 1, lambda j: above(j, lambda s: frame_copy(x, z, x_peer, 0, s).wait_send()))
+    each(deep, lambda s: frame_copy(x, z, x_peer, 1, s).wait_send())
     code_copy(c, c_peer).wait_send()
     for ch, side in ((0, x), (1, other)):
         each(half - 1, lambda k: stat_copy(ch, side, q_me, x_peer, k).wait_send())
@@ -348,7 +368,7 @@
             dma,
             dma,
             dma,
-            dma((2 * deep,)),
+            dma((2, deep)),
             dma((2, deep)),
             dma((2, half)),
             dma((half, 2)),
@@ -356,6 +376,7 @@
             dma((2 * reps,)),
             dma((half,)),
             dma((half,)),
+            pltpu.SemaphoreType.REGULAR((deep,)),
         ],
         compiler_params=pltpu.CompilerParams(collective_id=0, has_side_effects=True),
     )(frames, codebook)

time: 30.4 us -> 29.9 us (0.984)
  Pallas kernels: 26.8 us -> 26.3 us
    pallas_call x1, Pallas kernels: 26.8 us -> 26.3 us  [per_device(): pl.pallas_call(functools.partial(kernel, n, reps), out_shape=(OUT((1, blo...]
where the time goes in v4:
time: 29.9 us; the launch traced here: 29.7 us
  Pallas kernels  26.3 us (88%)
  between operations  2.33 us (8%)
  local copies, waits for them, and re-layouts  1.11 us (4%)
    pallas_call x1, Pallas kernels, per_device(): pl.pallas_call(functools.partial(kernel, n, reps), out_shape=(OUT((1, blo...  26.3 us
    unnamed x2, local copies, waits for them, and re-layouts  1.11 us

profile of v4, /device:TPU:0, one launch (start us, length us, event | category | flops | bytes accessed | tf_op | source)
XLA Modules:
  0.0 29.7 jit_solution(3341672297249311375)
XLA Ops:
  0.6 26.3 %shard_map.49 = (f32[1,48]{1,0:T(1,128)S(1)}, f32[1,1024]{1,0:T(1,128)S(1)}, f32[1,1]{1,0:T(1,128)}) custom-call(bf16[1,48,384]{2,1,0:T(8,128)(2,1)} %frame_hbm.1, bf16[1024,384]{1,0:T(8,128)(2,1)} %code_hbm.1), custom_call_target="tpu_custom_call" | custom-call | tf_op jit(solution)/shard_map/pallas_call | solution.py:341
  26.9 0.5 %copy.8 = f32[1,48]{1,0:T(1,128)} copy(f32[1,48]{1,0:T(1,128)S(1)} %get-tuple-element.9) | data formatting | bytes 384
  27.4 0.6 %copy.9 = f32[1024]{0:T(1024)} copy(f32[1024]{0:T(1024)S(1)} %bitcast.2) | data formatting | bytes 8192
